TPU v7x, 128 devices: a whole 4x4x4 slice. The times are simulated.
128 devices in a mesh: row: 8 (over y, core), col: 16 (over x, z).
Axes of the slice: x: 4, y: 4, z: 4, core: 2. Of those that a mesh axis runs over, the one named last changes fastest.
Arguments:
- b_tensor: bfloat16 [128, 1024, 1024], P('col', 'row'), may hold values from -6 to 6
- occ_green: bfloat16 [1024, 1024], P(('row', 'col')), may hold values from -0.1875 to 0.1875
- virt_green: bfloat16 [1024, 1024], P(('row', 'col')), may hold values from -0.1875 to 0.1875
- b_mask: int32 [1, 8, 8], replicated, may hold values 0 or 1
- occ_mask: int32 [8, 8], replicated, may hold values 0 or 1
- virt_mask: int32 [8, 8], replicated, may hold values 0 or 1
Outputs:
- chi: float32 [128, 128], P(('row', 'col'))
All inputs are finite; a program needn't handle non-finite values.
Results may differ from a plain program's by a relative error of at most 0.0041.
Values may be sent and summed in bfloat16 or wider, within the bound.
A program may use at most 64 MiB of HBM per device.

v0:
```python
import jax
import jax.numpy as jnp
from jax import lax
from jax.sharding import PartitionSpec as P

TILE = 128


def expand_pair(mask):
    return jnp.repeat(jnp.repeat(mask, TILE, axis=0), TILE, axis=1).astype(jnp.bfloat16)


def per_device(b_tensor, occ_green, virt_green, b_mask, occ_mask, virt_mask):
    col_index = lax.axis_index("col")
    row_index = lax.axis_index("row")
    p_count, m_count, n_basis = b_tensor.shape
    p_tiles = (col_index * p_count + jnp.arange(p_count, dtype=jnp.int32)) // TILE
    m_tiles = (row_index * m_count + jnp.arange(m_count, dtype=jnp.int32)) // TILE
    local_mask = jnp.take(jnp.take(b_mask, p_tiles, axis=0), m_tiles, axis=1).astype(jnp.bfloat16)
    masked = b_tensor * jnp.repeat(local_mask, TILE, axis=2)
    exchanged_b = lax.all_to_all(masked, "col", split_axis=2, concat_axis=0, tiled=True)
    virt_full = lax.all_gather(virt_green, ("row", "col"), axis=0, tiled=True) * expand_pair(
        virt_mask
    )
    occ_rows = lax.all_gather(occ_green, "col", axis=0, tiled=True)
    occ_rows = occ_rows * lax.dynamic_slice_in_dim(
        expand_pair(occ_mask), row_index * m_count, m_count, 0
    )
    inner = jnp.dot(masked.reshape(-1, n_basis), virt_full, preferred_element_type=jnp.float32)
    inner = inner.astype(jnp.bfloat16).reshape(masked.shape)
    outer = jnp.einsum(
        "lm,pms->pls",
        occ_rows,
        lax.all_gather(inner, "row", axis=1, tiled=True),
        preferred_element_type=jnp.float32,
    ).astype(jnp.bfloat16)
    moved = lax.all_to_all(outer, "col", split_axis=2, concat_axis=0, tiled=True)
    b_flat = exchanged_b.reshape(exchanged_b.shape[0], -1)
    y_flat = moved.reshape(moved.shape[0], -1)
    summed = lax.psum_scatter(
        lax.dot_general(
            y_flat, b_flat, (((1,), (1,)), ((), ())), preferred_element_type=jnp.float32
        ),
        ("row", "col"),
        scatter_dimension=0,
        tiled=True,
    )
    return summed * (-2.0 / n_basis)


def solution(mesh):
    return jax.shard_map(
        per_device,
        mesh=mesh,
        in_specs=(
            P("col", "row", None),
            P(("row", "col"), None),
            P(("row", "col"), None),
            P(),
            P(),
            P(),
        ),
        out_specs=P(("row", "col"), None),
        check_vma=False,
    )
```

profile of v0, /device:TPU:1, one launch (start us, length us, event | category | flops | bytes accessed | tf_op | source)
XLA Modules:
  0.0 387.0 jit_solution(18253904898014795396)
XLA Ops:
  6.5 0.0 all-gather.3.cloned.1.call-start
  6.5 0.7 all-gather.3.cloned.1.call-update
  7.3 0.0 all-gather.5.cloned.1.call-start
  7.4 0.8 broadcast_select_fusion
  8.1 0.8 gather_fusion
  8.9 0.2 fusion.3
  9.2 1.4 broadcast_in_dim.39
  10.5 0.0 copy-start.1
  10.5 2.3 reshape.157
  12.8 0.0 copy-done.1
  12.8 3.2 mul.24
  16.1 63.1 %all-gather.3.cloned.1.call-done = bf16[1024,1024]{1,0:T(8,128)(2,1)} async-done(((bf16[8,1024]{1,0:T(8,128)(2,1)}), bf16[1024,1024]{1,0:T(8,128)(2,1)}) %all-gather.3.cloned.1.call-update) | async-done | bytes 2097168 | tf_op jit(solution)/shard_map/all_gather | solution.py:22
  79.2 0.0 copy-start.3
  79.3 2.9 broadcast_in_dim.41
  82.2 0.0 copy-done.3
  82.2 3.7 fusion.2
  85.9 3.9 %copy.19 = bf16[8,128,1024]{1,2,0:T(8,128)(2,1)} copy(bf16[8,128,1024]{2,1,0:T(8,128)(2,1)} %bitcast.45) | data formatting | bytes 4194304 | tf_op jit(solution)/shard_map/reshape | solution.py:30
  89.8 0.0 all-gather.5.cloned.1.call-update
  89.9 2.9 copy.22
  92.8 0.0 copy-start.2
  92.8 4.2 %all-to-all-start.1 = ((bf16[8,128,1024]{1,0,2:T(8,128)(2,1)}), bf16[8,128,1024]{1,0,2:T(8,128)(2,1)S(1)}, u32[]{:S(2)}, u32[]{:S(2)}) async-start(bf16[8,128,1024]{1,0,2:T(8,128)(2,1)} %copy.22), calls=%async_computation.1 | async-start | bytes 4194304 | tf_op jit(solution)/shard_map/all_to_all | solution.py:21
  97.0 0.0 copy-done.2
  97.1 2.9 broadcast_in_dim.43
  100.0 0.0 copy-start
  100.1 2.0 copy.35
  102.0 0.0 copy-done
  102.0 36.4 %all_gather.11 = bf16[128,1024]{1,0:T(8,128)(2,1)S(1)} all-gather(bf16[8,1024]{1,0:T(8,128)(2,1)S(1)} %copy-done), channel_id=1, replica_groups=mesh['row'=8,'col'=16] {'col'}, dimensions={0}, use_global_device_ids=true | all-gather | bytes 278528 | tf_op jit(solution)/shard_map/all_gather | solution.py:25
  138.5 39.3 %all-gather.5.cloned.1.call-done = bf16[8,1024,1024]{1,2,0:T(8,128)(2,1)} async-done(((bf16[8,128,1024]{1,2,0:T(8,128)(2,1)}), bf16[8,1024,1024]{1,2,0:T(8,128)(2,1)}) %all-gather.5.cloned.1.call-update) | async-done | bytes 16777232 | tf_op jit(solution)/shard_map/all_gather | solution.py:34
  177.7 10.3 %convert_bitcast_fusion = bf16[8,128,1024]{1,2,0:T(8,128)(2,1)S(1)} fusion(bf16[8,1024,1024]{1,2,0:T(8,128)(2,1)} %all-gather.5.cloned.1.call-done, bf16[128,1024]{1,0:T(8,128)(2,1)S(1)} %all_gather.11, bf16[1024,1024]{1,0:T(8,128)(2,1)} %bitcast.44, s32[]{:T(128)S(6)} %select_n.83), kind=kOutput, calls=%fused_computation.5 | convolution fusion | flops 2149056512 | bytes 19398660 | tf_op jit(solution)/shard_map/lm,pms->pls/dot_general | solution.py:31
  188.0 2.7 copy.20
  190.7 0.0 all-to-all-done.1
  190.7 6.7 %all-to-all-start = ((bf16[8,128,1024]{1,0,2:T(8,128)(2,1)}), bf16[8,128,1024]{1,0,2:T(8,128)(2,1)}, u32[]{:S(2)}, u32[]{:S(2)}) async-start(bf16[8,128,1024]{1,0,2:T(8,128)(2,1)} %copy.20), calls=%async_computation | async-start | bytes 4194304 | tf_op jit(solution)/shard_map/all_to_all | solution.py:37
  197.5 0.0 all-reduce.3.cloned.1.call-start
  197.5 3.2 copy.24
  200.7 5.7 %reshape.161 = bf16[128,8192]{1,0:T(8,128)(2,1)S(1)} reshape(bf16[16,8,128,64]{3,2,1,0:T(8,128)(2,1)} %copy.24) | data formatting | bytes 4194304 | tf_op jit(solution)/shard_map/reshape | solution.py:38
  206.4 20.3 %all-to-all-done = bf16[8,128,1024]{1,0,2:T(8,128)(2,1)} async-done(((bf16[8,128,1024]{1,0,2:T(8,128)(2,1)}), bf16[8,128,1024]{1,0,2:T(8,128)(2,1)}, u32[]{:S(2)}, u32[]{:S(2)}) %all-to-all-start) | async-done | bytes 2097184 | tf_op jit(solution)/shard_map/all_to_all | solution.py:37
  226.7 4.8 %copy.21 = bf16[8,128,16,64]{3,1,0,2:T(8,128)(2,1)} copy(bf16[8,128,16,64]{1,0,3,2:T(8,128)(2,1)} %bitcast.9) | data formatting | bytes 4194304 | tf_op jit(solution)/shard_map/all_to_all | solution.py:37
  231.5 6.6 %reshape.160 = bf16[128,8192]{1,0:T(8,128)(2,1)} reshape(bf16[16,8,128,64]{3,2,1,0:T(8,128)(2,1)} %bitcast.39) | data formatting | bytes 4194304 | tf_op jit(solution)/shard_map/reshape | solution.py:39
  238.1 2.9 fusion.9
  241.1 0.0 all-reduce.3.cloned.1.call-update
  241.1 138.1 %all-reduce.3.cloned.1.call-done = f32[128,128]{1,0:T(8,128)} async-done(((f32[128,128]{1,0:T(8,128)}), f32[128,128]{1,0:T(8,128)}) %all-reduce.3.cloned.1.call-update) | async-done | bytes 65552
  379.2 1.2 dynamic-slice_multiply_fusion
  (9 shorter events, 0.2 us)
Async XLA Ops:
  6.5 72.7 %all-gather.3.cloned.1.call-start = ((), (), s32[]{:S(2)}) async-start(), calls=%async_computation.2 | async-start | bytes 2113536 | tf_op jit(solution)/shard_map/all_gather | solution.py:22
  7.3 170.5 %all-gather.5.cloned.1.call-start = ((), (), s32[]{:S(2)}) async-start(), calls=%async_computation.3 | async-start | bytes 18874368 | tf_op jit(solution)/shard_map/all_gather | solution.py:34
  10.5 2.3 copy-start.1
  79.2 3.0 copy-start.3
  92.8 4.2 %copy-start.2 = (s32[8,8]{1,0:T(8,128)S(1)}, s32[8,8]{1,0:T(8,128)}, u32[]{:S(2)}) copy-start(s32[8,8]{1,0:T(8,128)} %param.10) | copy-start | bytes 772
  92.8 97.9 %all-to-all-start.1 = ((bf16[8,128,1024]{1,0,2:T(8,128)(2,1)}), bf16[8,128,1024]{1,0,2:T(8,128)(2,1)S(1)}, u32[]{:S(2)}, u32[]{:S(2)}) async-start(bf16[8,128,1024]{1,0,2:T(8,128)(2,1)} %copy.22), calls=%async_computation.1 | async-start | bytes 4194304 | tf_op jit(solution)/shard_map/all_to_all | solution.py:21
  100.0 2.0 copy-start
  190.7 36.0 %all-to-all-start = ((bf16[8,128,1024]{1,0,2:T(8,128)(2,1)}), bf16[8,128,1024]{1,0,2:T(8,128)(2,1)}, u32[]{:S(2)}, u32[]{:S(2)}) async-start(bf16[8,128,1024]{1,0,2:T(8,128)(2,1)} %copy.20), calls=%async_computation | async-start | bytes 4194304 | tf_op jit(solution)/shard_map/all_to_all | solution.py:37
  197.5 181.8 %all-reduce.3.cloned.1.call-start = ((), (), s32[]{:S(2)}) async-start(), calls=%async_computation.4 | async-start | bytes 131072
Sparse Core Ops, SparseCore 0:
  10.3 68.8 all-gather.2
  90.0 87.6 all-gather.4
  241.2 137.9 all-reduce.2
where the time goes:
time: 388 us; the launch traced here: 387 us
  waiting for transfers between devices  262 us (68%)
  local copies, waits for them, and re-layouts  42.2 us (11%)
  blocking collectives  36.4 us (9%)
  matrix products  16.9 us (4%)
  between operations  13.3 us (3%)
  starting transfers between devices  11 us (3%)
  other arithmetic  5.47 us (1%)
    unnamed x4, waiting for transfers between devices  139 us
    all_gather x1, waiting for transfers between devices, per_device(): lax.all_gather(virt_green, ('row', 'col'), axis=0, tiled=True)  63.1 us
    all_gather x1, waiting for transfers between devices, per_device(): lax.all_gather(inner, 'row', axis=1, tiled=True)  39.3 us
    all_gather x1, blocking collectives, per_device(): occ_rows = lax.all_gather(occ_green, 'col', axis=0, tiled=True)  36.4 us
    all_to_all x1, waiting for transfers between devices, per_device(): lax.all_to_all(outer, 'col', split_axis=2, concat_axis=0, tiled=True)  20.3 us
    dot_general x1, matrix products, per_device(): jnp.einsum('lm,pms->pls', occ_rows, lax.all_gather(inner, 'row', axis=1,...  10.3 us
  transfers between devices with their start and end apart: 5, of which 4 were waited for; matrix products, arithmetic and copies ran while one was open for 10% of the time, Pallas kernels for 0%

commit v1 on v0

v1 whole, which is shorter than its diff:
```python
import functools

import jax
import jax.numpy as jnp
from jax import lax
from jax.experimental import pallas as pl
from jax.experimental.pallas import tpu as pltpu
from jax.sharding import PartitionSpec as P

TILE = 128
ROWS, COLS = 8, 16
DEVICES = ROWS * COLS
N = 1024
NP = 128
SUB = 8
F32, BF16 = jnp.float32, jnp.bfloat16


def to(row, col):
    return {"row": row, "col": col}


def send(src, dst, send_sem, recv_sem, row, col):
    pltpu.make_async_remote_copy(
        src_ref=src,
        dst_ref=dst,
        send_sem=send_sem,
        recv_sem=recv_sem,
        device_id=to(row, col),
        device_id_type=pl.DeviceIdType.MESH,
    ).start()


def wait(ref, sem):
    pltpu.make_async_copy(ref, ref, sem).wait()


def flat(pieces):
    return pieces.astype(F32).reshape(-1, pieces.shape[-1])


def lanes(mask_ref, *index):
    return jnp.concatenate(
        [jnp.full((1, TILE), mask_ref[(*index, j)].astype(F32)) for j in range(N // TILE)], axis=1
    )


def kernel(
    b_ref,
    occ_ref,
    virt_ref,
    b_mask,
    occ_mask,
    virt_mask,
    out_ref,
    gath,
    bp,
    bk,
    virt,
    occ,
    half,
    full,
    full_k,
    w,
    part,
    part_in,
    line,
    line_in,
    local_sem,
    ag_send,
    ag_recv,
    row_send,
    row_recv,
    col_send,
    col_recv,
    full_send,
    full_recv,
    red_send,
    red_recv,
):
    r, c = lax.axis_index("row"), lax.axis_index("col")
    y, k = r // 2, r % 2
    x, z = c // 4, c % 4
    me = r * COLS + c

    mate = r + 1 - 2 * k

    @pl.when(k == 0)
    def _():
        gath[0, r, x, z] = virt_ref[...]
        send(occ_ref, gath.at[1, r, x, z], ag_send.at[0], ag_recv.at[0], mate, c)

    @pl.when(k == 1)
    def _():
        gath[1, r, x, z] = occ_ref[...]
        send(virt_ref, gath.at[0, r, x, z], ag_send.at[0], ag_recv.at[0], mate, c)

    own_b = pltpu.make_async_copy(b_ref.at[r], bp.at[r], row_recv.at[0])
    own_b.start()

    @pl.loop(1, ROWS)
    def _(i):
        to_row = (r + i) % ROWS
        send(b_ref.at[to_row], bp.at[r], row_send, row_recv.at[i], to_row, c)

    wait(gath.at[0, 0, 0, 0], ag_recv.at[0])
    for i in range(1, 4):
        mine = gath.at[k, pl.ds(2 * y, 2), x, z]
        send(mine, mine, ag_send.at[1], ag_recv.at[1], 2 * ((y + i) % 4) + k, c)
    wait(gath.at[0, pl.ds(0, 6), 0, 0], ag_recv.at[1])
    mine2 = gath.at[k, :, x, z]
    for i in range(1, 4):
        to_col = jnp.where(k == 0, (x + i) % 4 * 4 + z, x * 4 + (z + i) % 4)
        send(mine2, mine2, ag_send.at[2], ag_recv.at[2], r, to_col)
    wait(gath.at[0, :, pl.ds(0, 3), 0], ag_recv.at[2])

    @pl.when(k == 0)
    def _():
        mine3 = gath.at[0, :, :, z]
        for i in range(1, 4):
            send(mine3, mine3, ag_send.at[3], ag_recv.at[3], r, x * 4 + (z + i) % 4)

    @pl.when(k == 1)
    def _():
        mine3 = gath.at[1, :, x]
        for i in range(1, 4):
            send(mine3, mine3, ag_send.at[3], ag_recv.at[3], r, (x + i) % 4 * 4 + z)

    wait(gath.at[0, :, pl.ds(0, 3)], ag_recv.at[3])
    send(gath.at[k], gath.at[k], ag_send.at[4], ag_recv.at[4], mate, c)

    own_k = pltpu.make_async_copy(b_ref.at[:, c], bk.at[pl.ds(c * 8, 8)], col_recv)
    own_k.start()

    @pl.loop(1, COLS)
    def _(j):
        to_col = (c + j) % COLS
        send(b_ref.at[:, to_col], bk.at[pl.ds(c * 8, 8)], col_send, col_recv, r, to_col)

    wait(gath.at[0], ag_recv.at[4])

    @pl.loop(0, ROWS)
    def _(i):
        rows = pl.ds(i * TILE, TILE)
        virt[rows, :] = (flat(gath[0, i].reshape(COLS, SUB, N)) * lanes(virt_mask, i)).astype(BF16)
        occ[rows, :] = (flat(gath[1, i].reshape(COLS, SUB, N)) * lanes(occ_mask, i)).astype(BF16)

    @pl.loop(0, ROWS)
    def _(i):
        src = (r + ROWS - i) % ROWS
        wait(bp.at[0], row_recv.at[i])
        masked = (flat(bp[src]) * lanes(b_mask, 0, src)).astype(BF16)
        rows = pl.ds(pl.multiple_of(src * TILE, TILE), TILE)
        half[rows, :] = jnp.dot(masked, virt[...], preferred_element_type=F32).astype(BF16)

    slot = ((c % 2) * 8 + r) * 8 + c // 2

    @pl.loop(0, ROWS)
    def _(i):
        block = (r + i) % ROWS
        rows = pl.ds(pl.multiple_of(block * TILE, TILE), TILE)
        done = jnp.dot(occ[rows, :], half[...], preferred_element_type=F32)
        done = done * lanes(b_mask, 0, block)
        full[pl.ds(block * COLS, COLS)] = done.reshape(COLS, SUB, N).astype(BF16)

        @pl.loop(0, COLS)
        def _(j):
            to_col = (c + j) % COLS
            piece = full.at[block * COLS + to_col]

            @pl.when(i + j > 0)
            def _():
                send(piece, full_k.at[slot], full_send, full_recv, block, to_col)

            @pl.when(i + j == 0)
            def _():
                pltpu.make_async_copy(piece, full_k.at[slot], full_recv).start()

    row_id = lax.broadcasted_iota(jnp.int32, (SUB, N), 0)
    col_id = lax.broadcasted_iota(jnp.int32, (SUB, N), 1)
    same = (row_id == col_id % SUB)[None]
    wait(bk, col_recv)
    wait(full_k, full_recv)
    right = flat(bk[...]).astype(BF16)
    for i in range(4):
        left = flat(full_k[pl.ds(i * 32, 32)]).astype(BF16)
        cross = lax.dot_general(left, right, (((1,), (1,)), ((), ())), preferred_element_type=F32)
        w[pl.ds(i * 32, 32), :] = jnp.sum(jnp.where(same, cross.reshape(32, SUB, N), 0.0), axis=1)
    pick = lax.broadcasted_iota(jnp.int32, (N, NP), 0) // SUB
    pick = (pick == lax.broadcasted_iota(jnp.int32, (N, NP), 1)).astype(F32)
    sums = jnp.dot(w[...], pick, preferred_element_type=F32, precision=lax.Precision.HIGHEST)
    part[...] = sums.reshape(COLS, ROWS, NP)

    own_part = pltpu.make_async_copy(part.at[c], part_in.at[c], red_recv.at[0])
    own_part.start()

    @pl.loop(1, COLS)
    def _(j):
        to_col = (c + j) % COLS
        send(part.at[to_col], part_in.at[c], red_send.at[0], red_recv.at[0], r, to_col)

    wait(part_in, red_recv.at[0])
    line[...] = jnp.sum(part_in[...], axis=0).reshape(ROWS, 1, NP)
    own_line = pltpu.make_async_copy(line.at[r], line_in.at[r], red_recv.at[1])
    own_line.start()

    @pl.loop(1, ROWS)
    def _(i):
        to_row = (r + i) % ROWS
        send(line.at[to_row], line_in.at[r], red_send.at[1], red_recv.at[1], to_row, c)

    wait(line_in, red_recv.at[1])
    out_ref[...] = jnp.sum(line_in[...], axis=0) * (-2.0 / N)

    wait(gath.at[0, 0, 0, 0], ag_send.at[0])
    wait(gath.at[0, pl.ds(0, 6), 0, 0], ag_send.at[1])
    wait(gath.at[0, :, pl.ds(0, 3), 0], ag_send.at[2])
    wait(gath.at[0, :, pl.ds(0, 3)], ag_send.at[3])
    wait(gath.at[0], ag_send.at[4])
    wait(bp.at[pl.ds(0, ROWS - 1)], row_send)
    wait(bk.at[pl.ds(0, 8 * (COLS - 1))], col_send)
    wait(full_k.at[pl.ds(0, DEVICES - 1)], full_send)
    wait(part_in.at[pl.ds(0, COLS - 1)], red_send.at[0])
    wait(line_in.at[pl.ds(0, ROWS - 1)], red_send.at[1])


def per_device(b_tensor, occ_green, virt_green, b_mask, occ_mask, virt_mask):
    vmem = pl.BlockSpec(memory_space=pltpu.VMEM)
    smem = pl.BlockSpec(memory_space=pltpu.SMEM)
    dma = pltpu.SemaphoreType.DMA
    return pl.pallas_call(
        kernel,
        out_shape=jax.ShapeDtypeStruct((1, NP), F32),
        in_specs=[pl.BlockSpec(memory_space=pl.ANY), vmem, vmem, smem, smem, smem],
        out_specs=vmem,
        scratch_shapes=[
            pltpu.VMEM((2, ROWS, 4, 4, SUB, N), BF16),
            pltpu.VMEM((ROWS, COLS, SUB, N), BF16),
            pltpu.VMEM((NP, SUB, N), BF16),
            pltpu.VMEM((N, N), BF16),
            pltpu.VMEM((N, N), BF16),
            pltpu.VMEM((N, N), BF16),
            pltpu.VMEM((DEVICES, SUB, N), BF16),
            pltpu.VMEM((NP, SUB, N), BF16),
            pltpu.VMEM((NP, N), F32),
            pltpu.VMEM((COLS, ROWS, NP), F32),
            pltpu.VMEM((COLS, ROWS, NP), F32),
            pltpu.VMEM((ROWS, 1, NP), F32),
            pltpu.VMEM((ROWS, 1, NP), F32),
            dma,
            dma((5,)),
            dma((5,)),
            dma,
            dma((ROWS,)),
            dma,
            dma,
            dma,
            dma,
            dma((2,)),
            dma((2,)),
        ],
        compiler_params=pltpu.CompilerParams(
            has_side_effects=True, vmem_limit_bytes=48 * 1024 * 1024
        ),
        name="chi",
    )(b_tensor.reshape(8, COLS, SUB, N), occ_green, virt_green, b_mask, occ_mask, virt_mask)


def solution(mesh):
    return jax.shard_map(
        per_device,
        mesh=mesh,
        in_specs=(
            P("col", "row", None),
            P(("row", "col"), None),
            P(("row", "col"), None),
            P(),
            P(),
            P(),
        ),
        out_specs=P(("row", "col"), None),
        check_vma=False,
    )
```

time: 388 us -> 142 us (0.37)
  waiting for transfers between devices: 262 us -> 0 us
  Pallas kernels: 0 us -> 136 us
  local copies, waits for them, and re-layouts: 42.2 us -> 5.6 us
  blocking collectives: 36.4 us -> 0 us
  matrix products: 16.9 us -> 0 us
  between operations: 13.3 us -> 0.02 us
  starting transfers between devices: 11 us -> 0 us
  other arithmetic: 5.47 us -> 0 us
    unnamed x4 -> x0, waiting for transfers between devices: 139 us -> none
    pallas_call x0 -> x1, Pallas kernels: none -> 136 us  [per_device(): pl.pallas_call(kernel, out_shape=jax.ShapeDtypeStruct((1, NP), F32), in_s...]
    all_gather x2 -> x0, waiting for transfers between devices: 102 us -> none  [the longest x1 63.1 us: per_device(): lax.all_gather(virt_green, ('row', 'col'), axis=0, tiled=True)]
    all_gather x1 -> x0, blocking collectives: 36.4 us -> none  [per_device(): occ_rows = lax.all_gather(occ_green, 'col', axis=0, tiled=True)]
    all_to_all x2 -> x0, waiting for transfers between devices: 20.3 us -> none  [the longest x1 20.3 us: per_device(): lax.all_to_all(outer, 'col', split_axis=2, concat_axis=0, tiled=True)]
    reshape x4 -> x0, local copies, waits for them, and re-layouts: 18.5 us -> none  [the longest x1 6.62 us: per_device(): y_flat = moved.reshape(moved.shape[0], -1)]
    dot_general x3 -> x0, matrix products: 16.9 us -> none  [the longest x1 10.3 us: per_device(): jnp.einsum('lm,pms->pls', occ_rows, lax.all_gather(inner, 'row', axis=1,...]
    all_to_all x2 -> x0, starting transfers between devices: 10.9 us -> none  [the longest x1 6.72 us: per_device(): lax.all_to_all(outer, 'col', split_axis=2, concat_axis=0, tiled=True)]
  transfers between devices with their start and end apart: 5 -> 0, of which waited for: 4 -> 0; matrix products, arithmetic and copies ran while one was open for 10% -> 0% of each run, Pallas kernels for 0% -> 0%
where the time goes in v1:
time: 142 us; the launch traced here: 141 us
  Pallas kernels  136 us (96%)
  local copies, waits for them, and re-layouts  5.6 us (4%)
    pallas_call x1, Pallas kernels, per_device(): pl.pallas_call(kernel, out_shape=jax.ShapeDtypeStruct((1, NP), F32), in_s...  136 us
    unnamed x13, local copies, waits for them, and re-layouts  5.6 us

profile of v1, /device:TPU:1, one launch (start us, length us, event | category | flops | bytes accessed | tf_op | source)
XLA Modules:
  0.0 141.2 jit_solution(18154874951612200351)
XLA Ops:
  0.0 0.0 copy-start
  0.0 1.6 %copy-done = bf16[8,128,1024]{2,1,0:T(8,128)(2,1)S(1)} copy-done((bf16[8,128,1024]{2,1,0:T(8,128)(2,1)S(1)}, bf16[8,128,1024]{2,1,0:T(8,128)(2,1)}, u32[]{:S(2)}) %copy-start) | copy-done | bytes 2097176
  1.6 0.0 copy-start.1
  1.6 0.7 copy-done.1
  2.3 0.0 copy-start.2
  2.3 0.7 copy-done.2
  3.0 0.0 copy-start.3
  3.0 0.7 copy-done.3
  3.7 0.0 copy-start.4
  3.7 0.7 copy-done.4
  4.4 0.0 copy-start.5
  4.4 0.7 copy-done.5
  5.1 135.6 %chi.1 = f32[1,128]{1,0:T(1,128)S(1)} custom-call(bf16[8,16,8,1024]{3,2,1,0:T(8,128)(2,1)S(1)} %bitcast.1, bf16[8,1024]{1,0:T(8,128)(2,1)S(1)} %copy-done.1, bf16[8,1024]{1,0:T(8,128)(2,1)S(1)} %copy-done.2, s32[1,8,8]{2,1,0:T(8,128)S(1)} %copy-done.3, s32[8,8]{1,0:T(8,128)S(1)} %copy-done.4, s32[8,8]{1,0:T(8,128)S(1)} %copy-done.5), custom_call_target="tpu_custom_call" | custom-call | tf_op jit(solution)/shard_map/chi/pallas_call | solution.py:231
  140.7 0.5 copy.8
Async XLA Ops:
  0.0 1.6 %copy-start = (bf16[8,128,1024]{2,1,0:T(8,128)(2,1)S(1)}, bf16[8,128,1024]{2,1,0:T(8,128)(2,1)}, u32[]{:S(2)}) copy-start(bf16[8,128,1024]{2,1,0:T(8,128)(2,1)} %param.6) | copy-start | bytes 6291460
  1.6 0.7 copy-start.1
  2.3 0.7 copy-start.2
  3.0 0.7 copy-start.3
  3.7 0.7 copy-start.4
  4.4 0.7 copy-start.5

commit v2 on v0

v2 whole, which is shorter than its diff:
```python
import jax
import jax.numpy as jnp
from jax import lax
from jax.experimental import pallas as pl
from jax.experimental.pallas import tpu as pltpu
from jax.sharding import PartitionSpec as P

TILE = 128
ROWS, COLS = 8, 16
DEVICES = ROWS * COLS
N = 1024
NP = 128
SUB = 8
GROUPS = 4
F32, BF16 = jnp.float32, jnp.bfloat16


def send(src, dst, send_sem, recv_sem, row, col):
    pltpu.make_async_remote_copy(
        src_ref=src,
        dst_ref=dst,
        send_sem=send_sem,
        recv_sem=recv_sem,
        device_id={"row": row, "col": col},
        device_id_type=pl.DeviceIdType.MESH,
    ).start()


def greet(sem, row, col):
    pl.semaphore_signal(
        sem, inc=1, device_id={"row": row, "col": col}, device_id_type=pl.DeviceIdType.MESH
    )


def wait(ref, sem):
    pltpu.make_async_copy(ref, ref, sem).wait()


def flat(pieces):
    return pieces.astype(F32).reshape(-1, N).astype(BF16)


def lanes(mask_ref, row):
    return jnp.concatenate(
        [jnp.full((1, TILE), mask_ref[row, j].astype(F32)) for j in range(N // TILE)], axis=1
    )


def kernel(
    b_hbm,
    occ_hbm,
    virt_hbm,
    b_mask_hbm,
    occ_mask_hbm,
    virt_mask_hbm,
    out_ref,
    b_mask,
    occ_mask,
    virt_mask,
    b,
    own,
    gath,
    bp,
    bk,
    virt,
    half,
    full,
    full_k,
    right,
    part,
    part_in,
    in_sem,
    b_sem,
    ag_send,
    ag_recv,
    mate_send,
    mate_recv,
    row_send,
    row_recv,
    col_send,
    col_recv,
    full_send,
    full_recv,
    red_send,
    red_recv,
):
    r, c = lax.axis_index("row"), lax.axis_index("col")
    y, k = r // 2, r % 2
    x, z = c // 4, c % 4
    me = r * COLS + c
    mate = r + 1 - 2 * k

    loads = [
        pltpu.make_async_copy(b_mask_hbm.at[0], b_mask, in_sem.at[0]),
        pltpu.make_async_copy(occ_mask_hbm, occ_mask, in_sem.at[1]),
        pltpu.make_async_copy(virt_mask_hbm, virt_mask, in_sem.at[2]),
        pltpu.make_async_copy(virt_hbm, own.at[0], in_sem.at[3]),
        pltpu.make_async_copy(occ_hbm, own.at[1], in_sem.at[4]),
    ]
    for load in loads:
        load.start()
    for p in range(8):
        pltpu.make_async_copy(b_hbm.at[p], b.at[p], b_sem.at[p]).start()

    barrier = pltpu.get_barrier_semaphore()
    for i in range(1, ROWS):
        greet(barrier, (r + i) % ROWS, c)
    for i in range(1, 4):
        greet(barrier, r, (x + i) % 4 * 4 + z)
        greet(barrier, r, x * 4 + (z + i) % 4)

    for load in loads:
        load.wait()
    own[0] = (own[0].astype(F32) * lanes(virt_mask, r)).astype(BF16)
    own[1] = (own[1].astype(F32) * lanes(occ_mask, r)).astype(BF16)
    keep = lanes(b_mask, r)[None]

    @pl.loop(0, 8)
    def _(p):
        wait(b.at[0], b_sem.at[p])
        b[p] = (b[p].astype(F32) * keep).astype(BF16)

    pl.semaphore_wait(barrier, ROWS - 1 + 6)

    for dk in range(2):
        to_k = (k + dk) % 2
        for dy in (0, 1, 3, 2):
            to_y = (y + dy) % 4
            if dy + dk:
                send(
                    own.at[to_k],
                    gath.at[to_k, y, k, x, z],
                    ag_send.at[0],
                    ag_recv.at[0],
                    to_y * 2 + to_k,
                    c,
                )
            else:
                pltpu.make_async_copy(own.at[k], gath.at[k, y, k, x, z], ag_recv.at[0]).start()

    for dk in range(2):
        for dy in (0, 1, 3, 2):
            to_row = (y + dy) % 4 * 2 + (k + dk) % 2
            if dy + dk:
                send(b.at[to_row], bp.at[r], row_send, row_recv.at[dy], to_row, c)
            else:
                pltpu.make_async_copy(b.at[r], bp.at[r], row_recv.at[0]).start()

    def by_columns(dx, dz):
        to_col = (x + dx) % 4 * 4 + (z + dz) % 4
        send(b.at[:, to_col], bk.at[pl.ds(c * 8, 8)], col_send, col_recv, r, to_col)

    pltpu.make_async_copy(b.at[:, c], bk.at[pl.ds(c * 8, 8)], col_recv).start()
    for i in (1, 3, 2):
        by_columns(0, i)
        by_columns(i, 0)

    wait(gath.at[0, :, :, 0, 0], ag_recv.at[0])
    line = gath.at[k, :, :, x, z]
    for i in (1, 3, 2):
        to_col = jnp.where(k == 0, (x + i) % 4 * 4 + z, x * 4 + (z + i) % 4)
        send(line, line, ag_send.at[1], ag_recv.at[1], r, to_col)
    wait(gath.at[0, :, :, pl.ds(0, 3), 0], ag_recv.at[1])

    @pl.when(k == 0)
    def _():
        plane = gath.at[0, :, :, :, z]
        for i in (1, 3, 2):
            send(plane, plane, ag_send.at[2], ag_recv.at[1 + i], r, x * 4 + (z + i) % 4)
        send(plane, plane, mate_send, mate_recv, mate, c)
        for i in (1, 3, 2):
            plane = gath.at[0, :, :, :, (z + 4 - i) % 4]
            wait(plane, ag_recv.at[1 + i])
            send(plane, plane, mate_send, mate_recv, mate, c)

    @pl.when(k == 1)
    def _():
        plane = gath.at[1, :, :, x]
        for i in (1, 3, 2):
            send(plane, plane, ag_send.at[2], ag_recv.at[1 + i], r, (x + i) % 4 * 4 + z)
        send(plane, plane, mate_send, mate_recv, mate, c)
        for i in (1, 3, 2):
            plane = gath.at[1, :, :, (x + 4 - i) % 4]
            wait(plane, ag_recv.at[1 + i])
            send(plane, plane, mate_send, mate_recv, mate, c)

    for u in range(4):
        for t in range(1, 4):
            if (t + u) % 4:
                by_columns(t, (t + u) % 4)

    wait(gath.at[0], mate_recv)

    for row in range(ROWS):
        virt[pl.ds(row * TILE, TILE), :] = flat(gath[0, row // 2, row % 2])
    for dy in (0, 1, 3, 2):
        from_y = (y + 4 - dy) % 4
        wait(bp.at[pl.ds(0, 2)], row_recv.at[dy])
        rows = pl.ds(pl.multiple_of(from_y * 256, 256), 256)
        block = flat(bp[pl.ds(from_y * 2, 2)])
        half[rows, :] = jnp.dot(block, virt[...], preferred_element_type=F32).astype(BF16)

    def offset(i):
        t = i % 4
        return t, (t + i // 16 % 4) % 4, (t + i // 4) % 4

    for dk in range(2):
        to_k = (k + dk) % 2
        done = jnp.dot(flat(gath[1, :, to_k]), half[...], preferred_element_type=F32)
        full[dk] = done.astype(BF16).reshape(4, COLS, SUB, N)

        @pl.loop(0, DEVICES // 2)
        def _(i):
            dx, dy, dz = offset(i)
            to_y, to_col = (y + dy) % 4, (x + dx) % 4 * 4 + (z + dz) % 4
            slot = dk * (DEVICES // 2) + i
            piece, arrived = full.at[dk, to_y, to_col], full_recv.at[slot // (NP // GROUPS)]

            def far():
                send(piece, full_k.at[slot], full_send, arrived, to_y * 2 + to_k, to_col)

            if dk:
                far()
            else:
                pl.when(i > 0)(far)

                @pl.when(i == 0)
                def _():
                    pltpu.make_async_copy(piece, full_k.at[0], arrived).start()

    wait(bk, col_recv)
    for row in range(ROWS):
        right[pl.ds(row * TILE, TILE), :] = flat(bk[pl.ds(row * COLS, COLS)])
    row_id = lax.broadcasted_iota(jnp.int32, (SUB, N), 0)
    col_id = lax.broadcasted_iota(jnp.int32, (SUB, N), 1)
    same = (row_id == col_id % SUB)[None]
    pick = lax.broadcasted_iota(jnp.int32, (N, NP), 0) // SUB
    pick = (pick == lax.broadcasted_iota(jnp.int32, (N, NP), 1)).astype(F32)
    size = NP // GROUPS
    for g in range(GROUPS):
        slots = pl.ds(g * size, size)
        wait(full_k.at[slots], full_recv.at[g])
        cross = lax.dot_general(
            flat(full_k[slots]), right[...], (((1,), (1,)), ((), ())), preferred_element_type=F32
        )
        kept = jnp.sum(jnp.where(same, cross.reshape(size, SUB, N), 0.0), axis=1)
        sums = jnp.dot(kept, pick, preferred_element_type=F32, precision=lax.Precision.HIGHEST)
        part[slots] = sums.reshape(size, 1, NP)

        @pl.loop(g * size, (g + 1) * size)
        def _(slot):
            dx, dy, dz = offset(slot % (DEVICES // 2))
            dk = slot // (DEVICES // 2)
            from_row = (y + 4 - dy) % 4 * 2 + (k + dk) % 2
            from_col = (x + 4 - dx) % 4 * 4 + (z + 4 - dz) % 4
            p = from_col * 8 + from_row

            @pl.when(p != me)
            def _():
                send(part.at[slot], part_in.at[me], red_send, red_recv, p // COLS, p % COLS)

            @pl.when(p == me)
            def _():
                pltpu.make_async_copy(part.at[slot], part_in.at[me], red_recv).start()

    wait(part_in, red_recv)
    out_ref[...] = jnp.sum(part_in[...], axis=0) * (-2.0 / N)

    wait(gath.at[0, :, :, 0, 0].at[pl.ds(0, 3)], ag_send.at[0])
    wait(gath.at[0, 0, 0, 0, 0], ag_send.at[0])
    wait(gath.at[0, :, :, pl.ds(0, 3), 0], ag_send.at[1])
    wait(gath.at[0, :, :, pl.ds(0, 3)], ag_send.at[2])
    wait(gath.at[0], mate_send)
    wait(bp.at[pl.ds(0, ROWS - 1)], row_send)
    wait(bk.at[pl.ds(0, 8 * (COLS - 1))], col_send)
    wait(full_k.at[pl.ds(0, DEVICES - 1)], full_send)
    wait(part_in.at[pl.ds(0, DEVICES - 1)], red_send)


def per_device(b_tensor, occ_green, virt_green, b_mask, occ_mask, virt_mask):
    hbm = pl.BlockSpec(memory_space=pltpu.HBM)
    dma = pltpu.SemaphoreType.DMA
    return pl.pallas_call(
        kernel,
        out_shape=jax.ShapeDtypeStruct((1, NP), F32),
        in_specs=[hbm] * 6,
        out_specs=pl.BlockSpec(memory_space=pltpu.VMEM),
        scratch_shapes=[
            pltpu.SMEM((8, 8), jnp.int32),
            pltpu.SMEM((8, 8), jnp.int32),
            pltpu.SMEM((8, 8), jnp.int32),
            pltpu.VMEM((8, COLS, SUB, N), BF16),
            pltpu.VMEM((2, SUB, N), BF16),
            pltpu.VMEM((2, 4, 2, 4, 4, SUB, N), BF16),
            pltpu.VMEM((ROWS, COLS, SUB, N), BF16),
            pltpu.VMEM((NP, SUB, N), BF16),
            pltpu.VMEM((N, N), BF16),
            pltpu.VMEM((N, N), BF16),
            pltpu.VMEM((2, 4, COLS, SUB, N), BF16),
            pltpu.VMEM((NP, SUB, N), BF16),
            pltpu.VMEM((N, N), BF16),
            pltpu.VMEM((NP, 1, NP), F32),
            pltpu.VMEM((DEVICES, 1, NP), F32),
            dma((5,)),
            dma((8,)),
            dma((3,)),
            dma((5,)),
            dma,
            dma,
            dma,
            dma((4,)),
            dma,
            dma,
            dma,
            dma((GROUPS,)),
            dma,
            dma,
        ],
        compiler_params=pltpu.CompilerParams(
            collective_id=0, has_side_effects=True, vmem_limit_bytes=48 * 1024 * 1024
        ),
        name="chi",
    )(b_tensor.reshape(8, COLS, SUB, N), occ_green, virt_green, b_mask, occ_mask, virt_mask)


def solution(mesh):
    return jax.shard_map(
        per_device,
        mesh=mesh,
        in_specs=(
            P("col", "row", None),
            P(("row", "col"), None),
            P(("row", "col"), None),
            P(),
            P(),
            P(),
        ),
        out_specs=P(("row", "col"), None),
        check_vma=False,
    )
```

time: 388 us -> 96.1 us (0.25)
  waiting for transfers between devices: 262 us -> 0 us
  Pallas kernels: 0 us -> 90.2 us
  local copies, waits for them, and re-layouts: 42.2 us -> 5.6 us
  blocking collectives: 36.4 us -> 0 us
  matrix products: 16.9 us -> 0 us
  between operations: 13.3 us -> 0.02 us
  starting transfers between devices: 11 us -> 0 us
  other arithmetic: 5.47 us -> 0 us
    unnamed x4 -> x0, waiting for transfers between devices: 139 us -> none
    all_gather x2 -> x0, waiting for transfers between devices: 102 us -> none  [the longest x1 63.1 us: per_device(): lax.all_gather(virt_green, ('row', 'col'), axis=0, tiled=True)]
    pallas_call x0 -> x1, Pallas kernels: none -> 90.2 us  [per_device(): pl.pallas_call(kernel, out_shape=jax.ShapeDtypeStruct((1, NP), F32), in_s...]
    all_gather x1 -> x0, blocking collectives: 36.4 us -> none  [per_device(): occ_rows = lax.all_gather(occ_green, 'col', axis=0, tiled=True)]
    all_to_all x2 -> x0, waiting for transfers between devices: 20.3 us -> none  [the longest x1 20.3 us: per_device(): lax.all_to_all(outer, 'col', split_axis=2, concat_axis=0, tiled=True)]
    reshape x4 -> x0, local copies, waits for them, and re-layouts: 18.5 us -> none  [the longest x1 6.62 us: per_device(): y_flat = moved.reshape(moved.shape[0], -1)]
    dot_general x3 -> x0, matrix products: 16.9 us -> none  [the longest x1 10.3 us: per_device(): jnp.einsum('lm,pms->pls', occ_rows, lax.all_gather(inner, 'row', axis=1,...]
    all_to_all x2 -> x0, starting transfers between devices: 10.9 us -> none  [the longest x1 6.72 us: per_device(): lax.all_to_all(outer, 'col', split_axis=2, concat_axis=0, tiled=True)]
  transfers between devices with their start and end apart: 5 -> 0, of which waited for: 4 -> 0; matrix products, arithmetic and copies ran while one was open for 10% -> 0% of each run, Pallas kernels for 0% -> 0%
where the time goes in v2:
time: 96.1 us; the launch traced here: 95.8 us
  Pallas kernels  90.2 us (94%)
  local copies, waits for them, and re-layouts  5.6 us (6%)
    pallas_call x1, Pallas kernels, per_device(): pl.pallas_call(kernel, out_shape=jax.ShapeDtypeStruct((1, NP), F32), in_s...  90.2 us
    unnamed x13, local copies, waits for them, and re-layouts  5.6 us

profile of v2, /device:TPU:1, one launch (start us, length us, event | category | flops | bytes accessed | tf_op | source)
XLA Modules:
  0.0 95.8 jit_solution(3118434932760399130)
XLA Ops:
  0.0 0.0 copy-start
  0.0 1.6 %copy-done = bf16[8,128,1024]{2,1,0:T(8,128)(2,1)S(1)} copy-done((bf16[8,128,1024]{2,1,0:T(8,128)(2,1)S(1)}, bf16[8,128,1024]{2,1,0:T(8,128)(2,1)}, u32[]{:S(2)}) %copy-start) | copy-done | bytes 2097176
  1.6 0.0 copy-start.1
  1.6 0.7 copy-done.1
  2.3 0.0 copy-start.2
  2.3 0.7 copy-done.2
  3.0 0.0 copy-start.3
  3.0 0.7 copy-done.3
  3.7 0.0 copy-start.4
  3.7 0.7 copy-done.4
  4.4 0.0 copy-start.5
  4.4 0.7 copy-done.5
  5.1 90.2 %chi.1 = f32[1,128]{1,0:T(1,128)S(1)} custom-call(bf16[8,16,8,1024]{3,2,1,0:T(8,128)(2,1)S(1)} %bitcast.1, bf16[8,1024]{1,0:T(8,128)(2,1)S(1)} %copy-done.1, bf16[8,1024]{1,0:T(8,128)(2,1)S(1)} %copy-done.2, s32[1,8,8]{2,1,0:T(8,128)S(1)} %copy-done.3, s32[8,8]{1,0:T(8,128)S(1)} %copy-done.4, s32[8,8]{1,0:T(8,128)S(1)} %copy-done.5), custom_call_target="tpu_custom_call" | custom-call | tf_op jit(solution)/shard_map/chi/pallas_call | solution.py:283
  95.3 0.5 copy.8
Async XLA Ops:
  0.0 1.6 %copy-start = (bf16[8,128,1024]{2,1,0:T(8,128)(2,1)S(1)}, bf16[8,128,1024]{2,1,0:T(8,128)(2,1)}, u32[]{:S(2)}) copy-start(bf16[8,128,1024]{2,1,0:T(8,128)(2,1)} %param.6) | copy-start | bytes 6291460
  1.6 0.7 copy-start.1
  2.3 0.7 copy-start.2
  3.0 0.7 copy-start.3
  3.7 0.7 copy-start.4
  4.4 0.7 copy-start.5

commit v3 on v2

--- a/solution.py
+++ b/solution.py
@@ -13,6 +13,7 @@
 SUB = 8
 GROUPS = 4
 F32, BF16 = jnp.float32, jnp.bfloat16
+rem, div = lax.rem, lax.div
 
 
 def send(src, dst, send_sem, recv_sem, row, col):
@@ -73,6 +74,9 @@
     b_sem,
     ag_send,
     ag_recv,
+    line_recv,
+    plane_recv,
+    ready,
     mate_send,
     mate_recv,
     row_send,
@@ -85,8 +89,8 @@
     red_recv,
 ):
     r, c = lax.axis_index("row"), lax.axis_index("col")
-    y, k = r // 2, r % 2
-    x, z = c // 4, c % 4
+    y, k = div(r, 2), rem(r, 2)
+    x, z = div(c, 4), rem(c, 4)
     me = r * COLS + c
     mate = r + 1 - 2 * k
 
@@ -104,10 +108,10 @@
 
     barrier = pltpu.get_barrier_semaphore()
     for i in range(1, ROWS):
-        greet(barrier, (r + i) % ROWS, c)
+        greet(barrier, rem(r + i, ROWS), c)
     for i in range(1, 4):
-        greet(barrier, r, (x + i) % 4 * 4 + z)
-        greet(barrier, r, x * 4 + (z + i) % 4)
+        greet(barrier, r, rem(x + i, 4) * 4 + z)
+        greet(barrier, r, x * 4 + rem(z + i, 4))
 
     for load in loads:
         load.wait()
@@ -122,111 +126,125 @@
 
     pl.semaphore_wait(barrier, ROWS - 1 + 6)
 
+    for i in range(1, 4):
+        greet(ready, r, rem(x + i, 4) * 4 + z)
+
+    a, b_at = jnp.where(k == 0, x, z), jnp.where(k == 0, z, x)
+
+    def along_a(i):
+        return jnp.where(k == 0, rem(x + i, 4) * 4 + z, x * 4 + rem(z + i, 4))
+
+    def along_b(i):
+        return jnp.where(k == 0, x * 4 + rem(z + i, 4), rem(x + i, 4) * 4 + z)
+
     for dk in range(2):
-        to_k = (k + dk) % 2
+        to_k = rem(k + dk, 2)
+        at = jnp.where(to_k == 0, x, z), jnp.where(to_k == 0, z, x)
         for dy in (0, 1, 3, 2):
-            to_y = (y + dy) % 4
             if dy + dk:
                 send(
                     own.at[to_k],
-                    gath.at[to_k, y, k, x, z],
+                    gath.at[to_k, y, k, *at],
                     ag_send.at[0],
-                    ag_recv.at[0],
-                    to_y * 2 + to_k,
+                    ag_recv,
+                    rem(y + dy, 4) * 2 + to_k,
                     c,
                 )
             else:
-                pltpu.make_async_copy(own.at[k], gath.at[k, y, k, x, z], ag_recv.at[0]).start()
+                pltpu.make_async_copy(own.at[k], gath.at[k, y, k, *at], ag_recv).start()
 
     for dk in range(2):
         for dy in (0, 1, 3, 2):
-            to_row = (y + dy) % 4 * 2 + (k + dk) % 2
+            to_row = rem(y + dy, 4) * 2 + rem(k + dk, 2)
             if dy + dk:
                 send(b.at[to_row], bp.at[r], row_send, row_recv.at[dy], to_row, c)
             else:
                 pltpu.make_async_copy(b.at[r], bp.at[r], row_recv.at[0]).start()
 
-    def by_columns(dx, dz):
-        to_col = (x + dx) % 4 * 4 + (z + dz) % 4
-        send(b.at[:, to_col], bk.at[pl.ds(c * 8, 8)], col_send, col_recv, r, to_col)
+    def by_columns(*steps):
+        for dx, dz in steps:
+            to_col = rem(x + dx, 4) * 4 + rem(z + dz, 4)
+            send(b.at[:, to_col], bk.at[pl.ds(c * 8, 8)], col_send, col_recv, r, to_col)
 
     pltpu.make_async_copy(b.at[:, c], bk.at[pl.ds(c * 8, 8)], col_recv).start()
-    for i in (1, 3, 2):
-        by_columns(0, i)
-        by_columns(i, 0)
-
-    wait(gath.at[0, :, :, 0, 0], ag_recv.at[0])
-    line = gath.at[k, :, :, x, z]
-    for i in (1, 3, 2):
-        to_col = jnp.where(k == 0, (x + i) % 4 * 4 + z, x * 4 + (z + i) % 4)
-        send(line, line, ag_send.at[1], ag_recv.at[1], r, to_col)
-    wait(gath.at[0, :, :, pl.ds(0, 3), 0], ag_recv.at[1])
-
-    @pl.when(k == 0)
-    def _():
-        plane = gath.at[0, :, :, :, z]
-        for i in (1, 3, 2):
-            send(plane, plane, ag_send.at[2], ag_recv.at[1 + i], r, x * 4 + (z + i) % 4)
-        send(plane, plane, mate_send, mate_recv, mate, c)
-        for i in (1, 3, 2):
-            plane = gath.at[0, :, :, :, (z + 4 - i) % 4]
-            wait(plane, ag_recv.at[1 + i])
-            send(plane, plane, mate_send, mate_recv, mate, c)
-
-    @pl.when(k == 1)
-    def _():
-        plane = gath.at[1, :, :, x]
-        for i in (1, 3, 2):
-            send(plane, plane, ag_send.at[2], ag_recv.at[1 + i], r, (x + i) % 4 * 4 + z)
-        send(plane, plane, mate_send, mate_recv, mate, c)
-        for i in (1, 3, 2):
-            plane = gath.at[1, :, :, (x + 4 - i) % 4]
-            wait(plane, ag_recv.at[1 + i])
-            send(plane, plane, mate_send, mate_recv, mate, c)
-
-    for u in range(4):
-        for t in range(1, 4):
-            if (t + u) % 4:
-                by_columns(t, (t + u) % 4)
-
+    by_columns((0, 1), (1, 0), (0, 3), (3, 0))
+
+    def line(j, q):
+        return gath.at[k, :, :, rem(a + 4 - j, 4), rem(b_at + q, 4)]
+
+    def on(ref):
+        send(ref, ref, mate_send, mate_recv, mate, c)
+
+    def spread(j):
+        send(line(j, 0), line(j, 0), ag_send.at[2], plane_recv.at[3, j], r, along_b(1))
+        send(line(j, 0), line(j, 0), ag_send.at[2], plane_recv.at[1, j], r, along_b(3))
+        on(line(j, 0))
+
+    def landed(j, q):
+        wait(line(j, q), plane_recv.at[q, j])
+        if q == 3 and j in (0, 1):
+            send(line(j, q), line(j, q), ag_send.at[2], plane_recv.at[2, j], r, along_b(1))
+        if q == 1 and j in (2, 3):
+            send(line(j, q), line(j, q), ag_send.at[2], plane_recv.at[2, j], r, along_b(3))
+        on(line(j, q))
+
+    wait(gath.at[0, :, :, 0, 0], ag_recv)
+    for j in (1, 3, 2):
+        send(line(0, 0), line(0, 0), ag_send.at[1], line_recv.at[j], r, along_a(j))
+    spread(0)
+    pl.semaphore_wait(ready, 3)
+    by_columns((0, 2), (2, 0), (1, 1), (3, 3), (1, 3), (3, 1))
+    for j in (1, 3):
+        wait(line(j, 0), line_recv.at[j])
+        spread(j)
+    landed(0, 3)
+    landed(0, 1)
+    wait(line(2, 0), line_recv.at[2])
+    spread(2)
+    by_columns((1, 2), (2, 1), (3, 2), (2, 3), (2, 2))
+    for j in (1, 3, 2):
+        landed(j, 3)
+        landed(j, 1)
+    for j in (0, 1, 3, 2):
+        landed(j, 2)
     wait(gath.at[0], mate_recv)
 
     for row in range(ROWS):
         virt[pl.ds(row * TILE, TILE), :] = flat(gath[0, row // 2, row % 2])
     for dy in (0, 1, 3, 2):
-        from_y = (y + 4 - dy) % 4
+        from_y = rem(y + 4 - dy, 4)
         wait(bp.at[pl.ds(0, 2)], row_recv.at[dy])
         rows = pl.ds(pl.multiple_of(from_y * 256, 256), 256)
         block = flat(bp[pl.ds(from_y * 2, 2)])
         half[rows, :] = jnp.dot(block, virt[...], preferred_element_type=F32).astype(BF16)
 
     def offset(i):
-        t = i % 4
-        return t, (t + i // 16 % 4) % 4, (t + i // 4) % 4
+        t = rem(i, 4)
+        return t, rem(t + div(i, 16) + 3, 4), rem(t + div(i, 4) + 3, 4)
 
     for dk in range(2):
-        to_k = (k + dk) % 2
+        to_k = rem(k + dk, 2)
         done = jnp.dot(flat(gath[1, :, to_k]), half[...], preferred_element_type=F32)
         full[dk] = done.astype(BF16).reshape(4, COLS, SUB, N)
 
         @pl.loop(0, DEVICES // 2)
         def _(i):
             dx, dy, dz = offset(i)
-            to_y, to_col = (y + dy) % 4, (x + dx) % 4 * 4 + (z + dz) % 4
+            to_y, to_x, to_z = rem(y + dy, 4), rem(x + dx, 4), rem(z + dz, 4)
             slot = dk * (DEVICES // 2) + i
-            piece, arrived = full.at[dk, to_y, to_col], full_recv.at[slot // (NP // GROUPS)]
+            piece, arrived = full.at[dk, to_y, to_z * 4 + to_x], full_recv.at[div(slot, NP // GROUPS)]
 
             def far():
-                send(piece, full_k.at[slot], full_send, arrived, to_y * 2 + to_k, to_col)
+                send(piece, full_k.at[slot], full_send, arrived, to_y * 2 + to_k, to_x * 4 + to_z)
 
             if dk:
                 far()
             else:
-                pl.when(i > 0)(far)
-
-                @pl.when(i == 0)
+                pl.when(i != 20)(far)
+
+                @pl.when(i == 20)
                 def _():
-                    pltpu.make_async_copy(piece, full_k.at[0], arrived).start()
+                    pltpu.make_async_copy(piece, full_k.at[20], arrived).start()
 
     wait(bk, col_recv)
     for row in range(ROWS):
@@ -249,15 +267,15 @@
 
         @pl.loop(g * size, (g + 1) * size)
         def _(slot):
-            dx, dy, dz = offset(slot % (DEVICES // 2))
-            dk = slot // (DEVICES // 2)
-            from_row = (y + 4 - dy) % 4 * 2 + (k + dk) % 2
-            from_col = (x + 4 - dx) % 4 * 4 + (z + 4 - dz) % 4
+            dx, dy, dz = offset(rem(slot, DEVICES // 2))
+            dk = (g * size) // (DEVICES // 2)
+            from_row = rem(y + 4 - dy, 4) * 2 + rem(k + dk, 2)
+            from_col = rem(x + 4 - dx, 4) * 4 + rem(z + 4 - dz, 4)
             p = from_col * 8 + from_row
 
             @pl.when(p != me)
             def _():
-                send(part.at[slot], part_in.at[me], red_send, red_recv, p // COLS, p % COLS)
+                send(part.at[slot], part_in.at[me], red_send, red_recv, div(p, COLS), rem(p, COLS))
 
             @pl.when(p == me)
             def _():
@@ -266,8 +284,8 @@
     wait(part_in, red_recv)
     out_ref[...] = jnp.sum(part_in[...], axis=0) * (-2.0 / N)
 
-    wait(gath.at[0, :, :, 0, 0].at[pl.ds(0, 3)], ag_send.at[0])
-    wait(gath.at[0, 0, 0, 0, 0], ag_send.at[0])
+    wait(own.at[0], ag_send.at[0])
+    wait(gath.at[0, pl.ds(0, 3), :, 0, 0], ag_send.at[0])
     wait(gath.at[0, :, :, pl.ds(0, 3), 0], ag_send.at[1])
     wait(gath.at[0, :, :, pl.ds(0, 3)], ag_send.at[2])
     wait(gath.at[0], mate_send)
@@ -304,7 +322,10 @@
             dma((5,)),
             dma((8,)),
             dma((3,)),
-            dma((5,)),
+            dma,
+            dma((4,)),
+            dma((4, 4)),
+            pltpu.SemaphoreType.REGULAR,
             dma,
             dma,
             dma,
@@ -317,7 +338,7 @@
             dma,
         ],
         compiler_params=pltpu.CompilerParams(
-            collective_id=0, has_side_effects=True, vmem_limit_bytes=48 * 1024 * 1024
+            collective_id=0, has_side_effects=True, vmem_limit_bytes=64 * 1024 * 1024 - 65536
         ),
         name="chi",
     )(b_tensor.reshape(8, COLS, SUB, N), occ_green, virt_green, b_mask, occ_mask, virt_mask)

time: 96.1 us -> 89 us (0.926)
  local copies, waits for them, and re-layouts: 5.6 us -> 1.19 us
  Pallas kernels: 90.2 us -> 87.7 us
    unnamed x13 -> x1, local copies, waits for them, and re-layouts: 5.6 us -> 1.19 us
    pallas_call x1, Pallas kernels: 90.2 us -> 87.7 us  [per_device(): pl.pallas_call(kernel, out_shape=jax.ShapeDtypeStruct((1, NP), F32), in_s...]
where the time goes in v3:
time: 89 us; the launch traced here: 88.9 us
  Pallas kernels  87.7 us (99%)
  local copies, waits for them, and re-layouts  1.19 us (1%)
    pallas_call x1, Pallas kernels, per_device(): pl.pallas_call(kernel, out_shape=jax.ShapeDtypeStruct((1, NP), F32), in_s...  87.7 us

profile of v3, /device:TPU:1, one launch (start us, length us, event | category | flops | bytes accessed | tf_op | source)
XLA Modules:
  0.0 88.9 jit_solution(16074362812768094565)
XLA Ops:
  0.0 87.7 %chi.1 = f32[1,128]{1,0:T(1,128)} custom-call(bf16[8,16,8,1024]{3,2,1,0:T(8,128)(2,1)} %bitcast.1, bf16[8,1024]{1,0:T(8,128)(2,1)} %occ_hbm.1, bf16[8,1024]{1,0:T(8,128)(2,1)} %virt_hbm.1, s32[1,8,8]{2,1,0:T(8,128)} %b_mask_hbm.1, s32[8,8]{1,0:T(8,128)} %occ_mask_hbm.1, s32[8,8]{1,0:T(8,128)} %virt_mask_hbm.1), custom_call_target="tpu_custom_call" | custom-call | tf_op jit(solution)/shard_map/chi/pallas_call | solution.py:301
  87.7 1.2 %copy.8 = f32[1,128]{1,0:T(1,128)} copy(f32[1,128]{1,0:T(1,128)} %chi.1) | data formatting | bytes 1024

commit v4 on v3

--- a/solution.py
+++ b/solution.py
@@ -139,19 +139,19 @@
 
     for dk in range(2):
         to_k = rem(k + dk, 2)
-        at = jnp.where(to_k == 0, x, z), jnp.where(to_k == 0, z, x)
+        at = jnp.where(to_k == 0, z, x), jnp.where(to_k == 0, x, z)
         for dy in (0, 1, 3, 2):
             if dy + dk:
                 send(
                     own.at[to_k],
-                    gath.at[to_k, y, k, *at],
+                    gath.at[to_k, *at, y, k],
                     ag_send.at[0],
                     ag_recv,
                     rem(y + dy, 4) * 2 + to_k,
                     c,
                 )
             else:
-                pltpu.make_async_copy(own.at[k], gath.at[k, y, k, *at], ag_recv).start()
+                pltpu.make_async_copy(own.at[k], gath.at[k, *at, y, k], ag_recv).start()
 
     for dk in range(2):
         for dy in (0, 1, 3, 2):
@@ -167,10 +167,10 @@
             send(b.at[:, to_col], bk.at[pl.ds(c * 8, 8)], col_send, col_recv, r, to_col)
 
     pltpu.make_async_copy(b.at[:, c], bk.at[pl.ds(c * 8, 8)], col_recv).start()
-    by_columns((0, 1), (1, 0), (0, 3), (3, 0))
+    by_columns((0, 1), (1, 0), (0, 3), (3, 0), (0, 2), (2, 0))
 
     def line(j, q):
-        return gath.at[k, :, :, rem(a + 4 - j, 4), rem(b_at + q, 4)]
+        return gath.at[k, rem(b_at + q, 4), rem(a + 4 - j, 4)]
 
     def on(ref):
         send(ref, ref, mate_send, mate_recv, mate, c)
@@ -188,12 +188,12 @@
             send(line(j, q), line(j, q), ag_send.at[2], plane_recv.at[2, j], r, along_b(3))
         on(line(j, q))
 
-    wait(gath.at[0, :, :, 0, 0], ag_recv)
+    wait(gath.at[0, 0, 0], ag_recv)
     for j in (1, 3, 2):
         send(line(0, 0), line(0, 0), ag_send.at[1], line_recv.at[j], r, along_a(j))
     spread(0)
     pl.semaphore_wait(ready, 3)
-    by_columns((0, 2), (2, 0), (1, 1), (3, 3), (1, 3), (3, 1))
+    by_columns((1, 1), (3, 3), (1, 3), (3, 1))
     for j in (1, 3):
         wait(line(j, 0), line_recv.at[j])
         spread(j)
@@ -201,16 +201,17 @@
     landed(0, 1)
     wait(line(2, 0), line_recv.at[2])
     spread(2)
-    by_columns((1, 2), (2, 1), (3, 2), (2, 3), (2, 2))
+    by_columns((1, 2), (3, 2))
     for j in (1, 3, 2):
         landed(j, 3)
         landed(j, 1)
     for j in (0, 1, 3, 2):
         landed(j, 2)
+    by_columns((2, 1), (2, 3), (2, 2))
     wait(gath.at[0], mate_recv)
 
     for row in range(ROWS):
-        virt[pl.ds(row * TILE, TILE), :] = flat(gath[0, row // 2, row % 2])
+        virt[pl.ds(row * TILE, TILE), :] = flat(jnp.swapaxes(gath[0, :, :, row // 2, row % 2], 0, 1))
     for dy in (0, 1, 3, 2):
         from_y = rem(y + 4 - dy, 4)
         wait(bp.at[pl.ds(0, 2)], row_recv.at[dy])
@@ -224,15 +225,21 @@
 
     for dk in range(2):
         to_k = rem(k + dk, 2)
-        done = jnp.dot(flat(gath[1, :, to_k]), half[...], preferred_element_type=F32)
-        full[dk] = done.astype(BF16).reshape(4, COLS, SUB, N)
+        done = jnp.dot(flat(gath[1, :, :, :, to_k]), half[...], preferred_element_type=F32)
+        full[dk] = done.astype(BF16).reshape(COLS, 4, SUB, N)
+
+    wait(bk, col_recv)
+    for row in range(ROWS):
+        right[pl.ds(row * TILE, TILE), :] = flat(bk[pl.ds(row * COLS, COLS)])
+    for dk in range(2):
+        to_k = rem(k + dk, 2)
 
         @pl.loop(0, DEVICES // 2)
         def _(i):
             dx, dy, dz = offset(i)
             to_y, to_x, to_z = rem(y + dy, 4), rem(x + dx, 4), rem(z + dz, 4)
             slot = dk * (DEVICES // 2) + i
-            piece, arrived = full.at[dk, to_y, to_z * 4 + to_x], full_recv.at[div(slot, NP // GROUPS)]
+            piece, arrived = full.at[dk, to_x * 4 + to_z, to_y], full_recv.at[div(slot, NP // GROUPS)]
 
             def far():
                 send(piece, full_k.at[slot], full_send, arrived, to_y * 2 + to_k, to_x * 4 + to_z)
@@ -246,9 +253,6 @@
                 def _():
                     pltpu.make_async_copy(piece, full_k.at[20], arrived).start()
 
-    wait(bk, col_recv)
-    for row in range(ROWS):
-        right[pl.ds(row * TILE, TILE), :] = flat(bk[pl.ds(row * COLS, COLS)])
     row_id = lax.broadcasted_iota(jnp.int32, (SUB, N), 0)
     col_id = lax.broadcasted_iota(jnp.int32, (SUB, N), 1)
     same = (row_id == col_id % SUB)[None]
@@ -285,9 +289,9 @@
     out_ref[...] = jnp.sum(part_in[...], axis=0) * (-2.0 / N)
 
     wait(own.at[0], ag_send.at[0])
-    wait(gath.at[0, pl.ds(0, 3), :, 0, 0], ag_send.at[0])
-    wait(gath.at[0, :, :, pl.ds(0, 3), 0], ag_send.at[1])
-    wait(gath.at[0, :, :, pl.ds(0, 3)], ag_send.at[2])
+    wait(gath.at[0, 0, 0, pl.ds(0, 3)], ag_send.at[0])
+    wait(gath.at[0, 0, pl.ds(0, 3)], ag_send.at[1])
+    wait(gath.at[0, pl.ds(0, 3)], ag_send.at[2])
     wait(gath.at[0], mate_send)
     wait(bp.at[pl.ds(0, ROWS - 1)], row_send)
     wait(bk.at[pl.ds(0, 8 * (COLS - 1))], col_send)
@@ -309,12 +313,12 @@
             pltpu.SMEM((8, 8), jnp.int32),
             pltpu.VMEM((8, COLS, SUB, N), BF16),
             pltpu.VMEM((2, SUB, N), BF16),
-            pltpu.VMEM((2, 4, 2, 4, 4, SUB, N), BF16),
+            pltpu.VMEM((2, 4, 4, 4, 2, SUB, N), BF16),
             pltpu.VMEM((ROWS, COLS, SUB, N), BF16),
             pltpu.VMEM((NP, SUB, N), BF16),
             pltpu.VMEM((N, N), BF16),
             pltpu.VMEM((N, N), BF16),
-            pltpu.VMEM((2, 4, COLS, SUB, N), BF16),
+            pltpu.VMEM((2, COLS, 4, SUB, N), BF16),
             pltpu.VMEM((NP, SUB, N), BF16),
             pltpu.VMEM((N, N), BF16),
             pltpu.VMEM((NP, 1, NP), F32),

time: 89 us -> 85.3 us (0.958)
  Pallas kernels: 87.7 us -> 84 us
    pallas_call x1, Pallas kernels: 87.7 us -> 84 us  [per_device(): pl.pallas_call(kernel, out_shape=jax.ShapeDtypeStruct((1, NP), F32), in_s...]
where the time goes in v4:
time: 85.3 us; the launch traced here: 85.2 us
  Pallas kernels  84 us (98%)
  local copies, waits for them, and re-layouts  1.19 us (1%)
    pallas_call x1, Pallas kernels, per_device(): pl.pallas_call(kernel, out_shape=jax.ShapeDtypeStruct((1, NP), F32), in_s...  84 us

profile of v4, /device:TPU:1, one launch (start us, length us, event | category | flops | bytes accessed | tf_op | source)
XLA Modules:
  0.0 85.2 jit_solution(4569754709283361552)
XLA Ops:
  0.0 84.0 %chi.1 = f32[1,128]{1,0:T(1,128)} custom-call(bf16[8,16,8,1024]{3,2,1,0:T(8,128)(2,1)} %bitcast.1, bf16[8,1024]{1,0:T(8,128)(2,1)} %occ_hbm.1, bf16[8,1024]{1,0:T(8,128)(2,1)} %virt_hbm.1, s32[1,8,8]{2,1,0:T(8,128)} %b_mask_hbm.1, s32[8,8]{1,0:T(8,128)} %occ_mask_hbm.1, s32[8,8]{1,0:T(8,128)} %virt_mask_hbm.1), custom_call_target="tpu_custom_call" | custom-call | tf_op jit(solution)/shard_map/chi/pallas_call | solution.py:305
  84.0 1.2 %copy.8 = f32[1,128]{1,0:T(1,128)} copy(f32[1,128]{1,0:T(1,128)} %chi.1) | data formatting | bytes 1024

commit v5 on v4

--- a/solution.py
+++ b/solution.py
@@ -198,10 +198,10 @@
         wait(line(j, 0), line_recv.at[j])
         spread(j)
     landed(0, 3)
+    by_columns((1, 2), (3, 2))
     landed(0, 1)
     wait(line(2, 0), line_recv.at[2])
     spread(2)
-    by_columns((1, 2), (3, 2))
     for j in (1, 3, 2):
         landed(j, 3)
         landed(j, 1)

time: 85.3 us -> 84.6 us (level)
  no operation moved by 1% of the time
where the time goes in v5:
time: 84.6 us; the launch traced here: 84.5 us
  Pallas kernels  83.3 us (98%)
  local copies, waits for them, and re-layouts  1.19 us (1%)
    pallas_call x1, Pallas kernels, per_device(): pl.pallas_call(kernel, out_shape=jax.ShapeDtypeStruct((1, NP), F32), in_s...  83.3 us

profile of v5, /device:TPU:1, one launch (start us, length us, event | category | flops | bytes accessed | tf_op | source)
XLA Modules:
  0.0 84.5 jit_solution(17692169164842196019)
XLA Ops:
  0.0 83.3 %chi.1 = f32[1,128]{1,0:T(1,128)} custom-call(bf16[8,16,8,1024]{3,2,1,0:T(8,128)(2,1)} %bitcast.1, bf16[8,1024]{1,0:T(8,128)(2,1)} %occ_hbm.1, bf16[8,1024]{1,0:T(8,128)(2,1)} %virt_hbm.1, s32[1,8,8]{2,1,0:T(8,128)} %b_mask_hbm.1, s32[8,8]{1,0:T(8,128)} %occ_mask_hbm.1, s32[8,8]{1,0:T(8,128)} %virt_mask_hbm.1), custom_call_target="tpu_custom_call" | custom-call | tf_op jit(solution)/shard_map/chi/pallas_call | solution.py:305
  83.3 1.2 %copy.8 = f32[1,128]{1,0:T(1,128)} copy(f32[1,128]{1,0:T(1,128)} %chi.1) | data formatting | bytes 1024

commit v6 on v5

--- a/solution.py
+++ b/solution.py
@@ -229,8 +229,6 @@
         full[dk] = done.astype(BF16).reshape(COLS, 4, SUB, N)
 
     wait(bk, col_recv)
-    for row in range(ROWS):
-        right[pl.ds(row * TILE, TILE), :] = flat(bk[pl.ds(row * COLS, COLS)])
     for dk in range(2):
         to_k = rem(k + dk, 2)
 
@@ -253,6 +251,8 @@
                 def _():
                     pltpu.make_async_copy(piece, full_k.at[20], arrived).start()
 
+    for row in range(ROWS):
+        right[pl.ds(row * TILE, TILE), :] = flat(bk[pl.ds(row * COLS, COLS)])
     row_id = lax.broadcasted_iota(jnp.int32, (SUB, N), 0)
     col_id = lax.broadcasted_iota(jnp.int32, (SUB, N), 1)
     same = (row_id == col_id % SUB)[None]

time: 84.6 us -> 84.6 us (level)
  no operation moved by 1% of the time
where the time goes in v6:
time: 84.6 us; the launch traced here: 84.5 us
  Pallas kernels  83.3 us (98%)
  local copies, waits for them, and re-layouts  1.19 us (1%)
    pallas_call x1, Pallas kernels, per_device(): pl.pallas_call(kernel, out_shape=jax.ShapeDtypeStruct((1, NP), F32), in_s...  83.3 us

profile of v6, /device:TPU:1, one launch (start us, length us, event | category | flops | bytes accessed | tf_op | source)
XLA Modules:
  0.0 84.5 jit_solution(10889759607102891688)
XLA Ops:
  0.0 83.3 %chi.1 = f32[1,128]{1,0:T(1,128)} custom-call(bf16[8,16,8,1024]{3,2,1,0:T(8,128)(2,1)} %bitcast.1, bf16[8,1024]{1,0:T(8,128)(2,1)} %occ_hbm.1, bf16[8,1024]{1,0:T(8,128)(2,1)} %virt_hbm.1, s32[1,8,8]{2,1,0:T(8,128)} %b_mask_hbm.1, s32[8,8]{1,0:T(8,128)} %occ_mask_hbm.1, s32[8,8]{1,0:T(8,128)} %virt_mask_hbm.1), custom_call_target="tpu_custom_call" | custom-call | tf_op jit(solution)/shard_map/chi/pallas_call | solution.py:305
  83.3 1.2 %copy.8 = f32[1,128]{1,0:T(1,128)} copy(f32[1,128]{1,0:T(1,128)} %chi.1) | data formatting | bytes 1024
